TPU v7x, 128 devices: a whole 4x4x4 slice. The times are simulated.
128 devices in a mesh: slab: 8 (over y, z_lo), row: 4 (over z_hi, core), col: 4 (over x).
Axes of the slice: x: 4, y: 4, z: 4 (z_hi: 2, z_lo: 2; z = z_hi * 2 + z_lo), core: 2. Of those that a mesh axis runs over, the one named last changes fastest.
Arguments:
- inverse: bfloat16 [8, 8192, 4, 2048], P('slab', 'row', None, 'col'), may hold values from -0.0625 to 0.0625
- sources: bfloat16 [8, 4, 8192, 128], P('slab', None, ('row', 'col')), may hold values from -6 to 6
- coupling: float32 [8, 2, 8192], P('slab', None, ('row', 'col')), may hold values from -1 to 1
- plan: int32 [6, 8, 2], replicated, may hold values from 0 to 3
Outputs:
- up_out: bfloat16 [8, 8192, 128], P('slab', ('row', 'col'))
- down_out: bfloat16 [8, 8192, 128], P('slab', ('row', 'col'))
Inputs may be any that keep to these rules, and one draw needn't show every extreme that they name: `plan`: each entry names one of the 4 stored batches of its slab.
All inputs are finite; a program needn't handle non-finite values.
Results may differ from a plain program's by a relative error of at most 0.023.
Values may be sent and summed in bfloat16 or wider, within the bound.
No kernel may reach another device: no remote copies, remote signals or barrier semaphores. Data moves between devices by JAX's collectives and lax.ppermute only.
A program may use at most 64 MiB of HBM per device.

v0:
```python
import jax
import jax.numpy as jnp
from jax import lax
from jax.sharding import PartitionSpec as P

TICKS = 6


def in_blocks(value, dim, count):
    lengths = value.shape
    pieces = value.reshape(*lengths[:dim], count, lengths[dim] // count, *lengths[dim + 1 :])
    return jnp.moveaxis(pieces, dim, 0)


def summed_on_arrival(value, axis, dim):
    count = lax.axis_size(axis)
    pieces = lax.all_to_all(in_blocks(value, dim, count), axis, 0, 0, tiled=True)
    return jnp.sum(pieces.astype(jnp.float32), axis=0)


def from_everyone(value, axis):
    count = lax.axis_size(axis)
    return lax.all_to_all(
        jnp.broadcast_to(value[None], (count, *value.shape)), axis, 0, 0, tiled=True
    )


def laid_out(pieces, dim):
    lengths = list(pieces.shape[1:])
    lengths[dim] *= pieces.shape[0]
    return jnp.moveaxis(pieces, 0, dim).reshape(lengths)


def collect(value, axis, dim):
    pieces = from_everyone(value, axis)
    return laid_out(pieces, dim)


def shifted(value, axis, steps):
    count = lax.axis_size(axis)
    leading, last = (max(0, -steps), min(count, count - steps))
    return lax.ppermute(value, axis, [(source, source + steps) for source in range(leading, last)])


def per_device(inverse, sources, coupling, plan):
    local_block = inverse[0]
    rows_here = local_block.shape[0]
    matrix = local_block.reshape(rows_here, -1)
    piece_rows = sources.shape[2]
    batch_width = sources.shape[3]
    slab_index = lax.axis_index("slab")
    up_gain = coupling[0, 0][:, None]
    down_gain = coupling[0, 1][:, None]
    stored = sources[0]
    up_out = jnp.zeros((piece_rows, batch_width), jnp.bfloat16)
    down_out = jnp.zeros((piece_rows, batch_width), jnp.bfloat16)
    for tick_index in range(TICKS):
        if tick_index == 0:
            up_recv = up_out
            down_recv = down_out
        else:
            up_recv = shifted(up_out, "slab", 1)
            down_recv = shifted(down_out, "slab", -1)
        up_choice = plan[tick_index, slab_index, 0]
        down_choice = plan[tick_index, slab_index, 1]
        up_source = lax.dynamic_index_in_dim(stored, up_choice, 0, keepdims=False)
        down_source = lax.dynamic_index_in_dim(stored, down_choice, 0, keepdims=False)
        up_in = (up_source.astype(jnp.float32) + up_gain * up_recv.astype(jnp.float32)).astype(
            jnp.bfloat16
        )
        down_in = (
            down_source.astype(jnp.float32) + down_gain * down_recv.astype(jnp.float32)
        ).astype(jnp.bfloat16)
        forward_partial_value = jnp.dot(
            matrix,
            lax.all_gather(up_in, "row", axis=0, tiled=True),
            preferred_element_type=jnp.float32,
        )
        forward_summed = summed_on_arrival(forward_partial_value.astype(jnp.bfloat16), "col", 0)
        up_out = forward_summed.astype(jnp.bfloat16)
        partial_value = lax.dot_general(
            matrix,
            collect(down_in, "col", 0),
            (((0,), (0,)), ((), ())),
            preferred_element_type=jnp.float32,
        )
        summed = summed_on_arrival(partial_value.astype(jnp.bfloat16), "row", 0)
        down_out = summed.astype(jnp.bfloat16)
    return (up_out[None], down_out[None])


def solution(mesh):
    placed = (
        P("slab", "row", None, "col"),
        P("slab", None, ("row", "col"), None),
        P("slab", None, ("row", "col")),
        P(),
    )
    return jax.shard_map(
        per_device,
        mesh=mesh,
        in_specs=placed,
        out_specs=(P("slab", ("row", "col"), None), P("slab", ("row", "col"), None)),
        check_vma=False,
    )
```

profile of v0, /device:TPU:16, one launch (start us, length us, event | category | flops | bytes accessed | tf_op | source)
XLA Modules:
  0.0 361.2 jit_solution(5221047215801752886)
XLA Ops:
  8.6 4.3 %all-to-all-start.6 = ((bf16[4,512,128]{2,1,0:T(8,128)(2,1)}), bf16[4,512,128]{2,1,0:T(8,128)(2,1)S(1)}, u32[]{:S(2)}, u32[]{:S(2)}) async-start(bf16[4,512,128]{2,1,0:T(8,128)(2,1)} %broadcast_in_dim.17), calls=%async_computation.6 | async-start | bytes 1048576 | tf_op jit(solution)/shard_map/all_to_all | solution.py:23
  12.9 9.5 %all_gather.18 = bf16[2048,128]{1,0:T(8,128)(2,1)S(1)} all-gather(bf16[512,128]{1,0:T(8,128)(2,1)S(1)} %get-tuple-element.15), channel_id=1, replica_groups=mesh['slab'=8,'row'=4,'col'=4] {'row'}, dimensions={0}, use_global_device_ids=true | all-gather | bytes 655360 | tf_op jit(solution)/shard_map/all_gather | solution.py:76
  22.4 10.2 %copy.81 = bf16[256,8,4,512]{3,1,2,0:T(8,128)(2,1)} copy(bf16[256,8,4,512]{3,2,1,0:T(4,128)(2,1)} %bitcast.157) | data formatting | bytes 16777216
  32.6 6.3 %convolution_convert_fusion.11 = bf16[128,2048]{1,0:T(8,128)(2,1)S(1)} fusion(bf16[2048,128]{1,0:T(8,128)(2,1)S(1)} %all_gather.18, bf16[2048,2048]{1,0:T(8,128)(2,1)} %bitcast.145), kind=kOutput, calls=%fused_computation.11 | convolution fusion | flops 1074003968 | bytes 9437184 | tf_op jit(solution)/shard_map/dot_general | solution.py:74
  39.8 4.8 %all-to-all-start = ((bf16[4,512,128]{1,2,0:T(8,128)(2,1)}), bf16[4,512,128]{1,2,0:T(8,128)(2,1)S(1)}, u32[]{:S(2)}, u32[]{:S(2)}) async-start(bf16[4,512,128]{1,2,0:T(8,128)(2,1)} %bitcast.144), calls=%async_computation | async-start | bytes 1048576 | tf_op jit(solution)/shard_map/all_to_all | solution.py:17
  44.7 4.7 %convolution_convert_fusion.5 = bf16[128,2048]{1,0:T(8,128)(2,1)S(1)} fusion(bf16[2048,128]{1,0:T(8,128)(2,1)S(1)} %bitcast.158, bf16[2048,2048]{1,0:T(8,128)(2,1)} %bitcast.146), kind=kOutput, calls=%fused_computation.5 | convolution fusion | flops 1074003968 | bytes 9437184 | tf_op jit(solution)/shard_map/dot_general | solution.py:81
  50.2 4.4 %all-to-all-done = bf16[4,512,128]{1,2,0:T(8,128)(2,1)S(1)} async-done(((bf16[4,512,128]{1,2,0:T(8,128)(2,1)}), bf16[4,512,128]{1,2,0:T(8,128)(2,1)S(1)}, u32[]{:S(2)}, u32[]{:S(2)}) %all-to-all-start) | async-done | bytes 524320 | tf_op jit(solution)/shard_map/all_to_all | solution.py:17
  54.6 3.6 all-to-all-start.7
  76.7 2.9 collective-permute-start
  80.1 5.4 %collective-permute-done = bf16[512,128]{0,1:T(8,128)(2,1)S(1)} collective-permute-done((bf16[512,128]{0,1:T(8,128)(2,1)S(1)}, bf16[512,128]{0,1:T(8,128)(2,1)S(1)}, u32[]{:S(2)}, u32[]{:S(2)}) %collective-permute-start) | collective-permute-done | bytes 131104 | tf_op jit(solution)/shard_map/ppermute | solution.py:42
  85.6 1.9 collective-permute-start.5
  87.5 11.0 %all_gather.19 = bf16[2048,128]{0,1:T(8,128)(2,1)S(1)} all-gather(bf16[512,128]{0,1:T(8,128)(2,1)S(1)} %fusion.7), channel_id=1, replica_groups=mesh['slab'=8,'row'=4,'col'=4] {'row'}, dimensions={0}, use_global_device_ids=true | all-gather | bytes 655360 | tf_op jit(solution)/shard_map/all_gather | solution.py:76
  99.6 3.5 all-to-all-start.8
  103.1 6.3 %convolution_convert_fusion.10 = bf16[128,2048]{1,0:T(8,128)(2,1)S(1)} fusion(bf16[2048,128]{0,1:T(8,128)(2,1)S(1)} %all_gather.19, bf16[2048,2048]{1,0:T(8,128)(2,1)} %bitcast.147), kind=kOutput, calls=%fused_computation.10 | convolution fusion | flops 1074003968 | bytes 9437184 | tf_op jit(solution)/shard_map/dot_general | solution.py:74
  110.2 3.1 all-to-all-done.8
  113.3 3.6 %all-to-all-start.1 = ((bf16[4,512,128]{1,2,0:T(8,128)(2,1)}), bf16[4,512,128]{1,2,0:T(8,128)(2,1)S(1)}, u32[]{:S(2)}, u32[]{:S(2)}) async-start(bf16[4,512,128]{1,2,0:T(8,128)(2,1)} %bitcast.143), calls=%async_computation.1 | async-start | bytes 1048576 | tf_op jit(solution)/shard_map/all_to_all | solution.py:17
  117.0 4.7 %convolution_convert_fusion.4 = bf16[128,2048]{1,0:T(8,128)(2,1)S(1)} fusion(bf16[2048,128]{1,0:T(8,128)(2,1)S(1)} %bitcast.160, bf16[2048,2048]{1,0:T(8,128)(2,1)} %bitcast.148), kind=kOutput, calls=%fused_computation.4 | convolution fusion | flops 1074003968 | bytes 9437184 | tf_op jit(solution)/shard_map/dot_general | solution.py:81
  122.5 3.7 %all-to-all-done.1 = bf16[4,512,128]{1,2,0:T(8,128)(2,1)S(1)} async-done(((bf16[4,512,128]{1,2,0:T(8,128)(2,1)}), bf16[4,512,128]{1,2,0:T(8,128)(2,1)S(1)}, u32[]{:S(2)}, u32[]{:S(2)}) %all-to-all-start.1) | async-done | bytes 524320 | tf_op jit(solution)/shard_map/all_to_all | solution.py:17
  126.2 3.5 all-to-all-start.9
  129.7 2.0 collective-permute-start.1
  132.0 7.2 %collective-permute-done.1 = bf16[512,128]{0,1:T(8,128)(2,1)S(1)} collective-permute-done((bf16[512,128]{0,1:T(8,128)(2,1)S(1)}, bf16[512,128]{0,1:T(8,128)(2,1)S(1)}, u32[]{:S(2)}, u32[]{:S(2)}) %collective-permute-start.1) | collective-permute-done | bytes 131104 | tf_op jit(solution)/shard_map/ppermute | solution.py:42
  140.6 4.1 %collective-permute-start.6 = (bf16[512,128]{0,1:T(8,128)(2,1)S(1)}, bf16[512,128]{0,1:T(8,128)(2,1)S(1)}, u32[]{:S(2)}, u32[]{:S(2)}) collective-permute-start(bf16[512,128]{0,1:T(8,128)(2,1)S(1)} %reduce_sum.151), channel_id=1, source_target_pairs={{16,0},{32,16},{48,32},{64,48},{80,64},{96,80},{112,96},{17,1},{33... | collective-permute-start | bytes 393224 | tf_op jit(solution)/shard_map/ppermute | solution.py:42
  144.7 9.6 %all_gather.20 = bf16[2048,128]{0,1:T(8,128)(2,1)S(1)} all-gather(bf16[512,128]{0,1:T(8,128)(2,1)S(1)} %fusion.8), channel_id=1, replica_groups=mesh['slab'=8,'row'=4,'col'=4] {'row'}, dimensions={0}, use_global_device_ids=true | all-gather | bytes 655360 | tf_op jit(solution)/shard_map/all_gather | solution.py:76
  155.4 3.5 all-to-all-start.10
  158.8 6.3 %convolution_convert_fusion.9 = bf16[128,2048]{1,0:T(8,128)(2,1)S(1)} fusion(bf16[2048,128]{0,1:T(8,128)(2,1)S(1)} %all_gather.20, bf16[2048,2048]{1,0:T(8,128)(2,1)} %bitcast.149), kind=kOutput, calls=%fused_computation.9 | convolution fusion | flops 1074003968 | bytes 9437184 | tf_op jit(solution)/shard_map/dot_general | solution.py:74
  166.0 3.1 all-to-all-done.10
  169.1 3.5 all-to-all-start.2
  172.6 4.7 %convolution_convert_fusion.3 = bf16[128,2048]{1,0:T(8,128)(2,1)S(1)} fusion(bf16[2048,128]{1,0:T(8,128)(2,1)S(1)} %bitcast.161, bf16[2048,2048]{1,0:T(8,128)(2,1)} %bitcast.150), kind=kOutput, calls=%fused_computation.3 | convolution fusion | flops 1074003968 | bytes 9437184 | tf_op jit(solution)/shard_map/dot_general | solution.py:81
  178.1 3.8 %all-to-all-done.2 = bf16[4,512,128]{1,2,0:T(8,128)(2,1)S(1)} async-done(((bf16[4,512,128]{1,2,0:T(8,128)(2,1)}), bf16[4,512,128]{1,2,0:T(8,128)(2,1)S(1)}, u32[]{:S(2)}, u32[]{:S(2)}) %all-to-all-start.2) | async-done | bytes 524320 | tf_op jit(solution)/shard_map/all_to_all | solution.py:17
  181.9 3.5 all-to-all-start.11
  185.5 1.9 collective-permute-start.2
  187.7 7.2 %collective-permute-done.2 = bf16[512,128]{0,1:T(8,128)(2,1)S(1)} collective-permute-done((bf16[512,128]{0,1:T(8,128)(2,1)S(1)}, bf16[512,128]{0,1:T(8,128)(2,1)S(1)}, u32[]{:S(2)}, u32[]{:S(2)}) %collective-permute-start.2) | collective-permute-done | bytes 131104 | tf_op jit(solution)/shard_map/ppermute | solution.py:42
  196.4 2.8 collective-permute-start.7
  199.2 10.9 %all_gather.21 = bf16[2048,128]{0,1:T(8,128)(2,1)S(1)} all-gather(bf16[512,128]{0,1:T(8,128)(2,1)S(1)} %fusion.9), channel_id=1, replica_groups=mesh['slab'=8,'row'=4,'col'=4] {'row'}, dimensions={0}, use_global_device_ids=true | all-gather | bytes 655360 | tf_op jit(solution)/shard_map/all_gather | solution.py:76
  211.1 3.5 all-to-all-start.12
  214.6 6.3 %convolution_convert_fusion.8 = bf16[128,2048]{1,0:T(8,128)(2,1)S(1)} fusion(bf16[2048,128]{0,1:T(8,128)(2,1)S(1)} %all_gather.21, bf16[2048,2048]{1,0:T(8,128)(2,1)} %bitcast.151), kind=kOutput, calls=%fused_computation.8 | convolution fusion | flops 1074003968 | bytes 9437184 | tf_op jit(solution)/shard_map/dot_general | solution.py:74
  221.7 3.1 all-to-all-done.12
  224.8 3.5 all-to-all-start.3
  228.3 4.7 %convolution_convert_fusion.2 = bf16[128,2048]{1,0:T(8,128)(2,1)S(1)} fusion(bf16[2048,128]{1,0:T(8,128)(2,1)S(1)} %bitcast.162, bf16[2048,2048]{1,0:T(8,128)(2,1)} %bitcast.152), kind=kOutput, calls=%fused_computation.2 | convolution fusion | flops 1074003968 | bytes 9437184 | tf_op jit(solution)/shard_map/dot_general | solution.py:81
  233.9 3.8 %all-to-all-done.3 = bf16[4,512,128]{1,2,0:T(8,128)(2,1)S(1)} async-done(((bf16[4,512,128]{1,2,0:T(8,128)(2,1)}), bf16[4,512,128]{1,2,0:T(8,128)(2,1)S(1)}, u32[]{:S(2)}, u32[]{:S(2)}) %all-to-all-start.3) | async-done | bytes 524320 | tf_op jit(solution)/shard_map/all_to_all | solution.py:17
  237.7 3.5 all-to-all-start.13
  241.3 1.9 collective-permute-start.3
  243.4 7.2 %collective-permute-done.3 = bf16[512,128]{0,1:T(8,128)(2,1)S(1)} collective-permute-done((bf16[512,128]{0,1:T(8,128)(2,1)S(1)}, bf16[512,128]{0,1:T(8,128)(2,1)S(1)}, u32[]{:S(2)}, u32[]{:S(2)}) %collective-permute-start.3) | collective-permute-done | bytes 131104 | tf_op jit(solution)/shard_map/ppermute | solution.py:42
  252.1 1.9 collective-permute-start.8
  254.0 10.5 %all_gather.22 = bf16[2048,128]{0,1:T(8,128)(2,1)S(1)} all-gather(bf16[512,128]{0,1:T(8,128)(2,1)S(1)} %fusion.10), channel_id=1, replica_groups=mesh['slab'=8,'row'=4,'col'=4] {'row'}, dimensions={0}, use_global_device_ids=true | all-gather | bytes 655360 | tf_op jit(solution)/shard_map/all_gather | solution.py:76
  265.6 3.7 %all-to-all-start.14 = ((bf16[4,512,128]{2,1,0:T(8,128)(2,1)}), bf16[4,512,128]{2,1,0:T(8,128)(2,1)S(1)}, u32[]{:S(2)}, u32[]{:S(2)}) async-start(bf16[4,512,128]{2,1,0:T(8,128)(2,1)} %broadcast_in_dim.21), calls=%async_computation.14 | async-start | bytes 1048576 | tf_op jit(solution)/shard_map/all_to_all | solution.py:23
  269.3 6.3 %convolution_convert_fusion.7 = bf16[128,2048]{1,0:T(8,128)(2,1)S(1)} fusion(bf16[2048,128]{0,1:T(8,128)(2,1)S(1)} %all_gather.22, bf16[2048,2048]{1,0:T(8,128)(2,1)} %bitcast.153), kind=kOutput, calls=%fused_computation.7 | convolution fusion | flops 1074003968 | bytes 9437184 | tf_op jit(solution)/shard_map/dot_general | solution.py:74
  276.5 2.9 all-to-all-done.14
  279.3 3.5 all-to-all-start.4
  282.8 4.7 %convolution_convert_fusion.1 = bf16[128,2048]{1,0:T(8,128)(2,1)S(1)} fusion(bf16[2048,128]{1,0:T(8,128)(2,1)S(1)} %bitcast.163, bf16[2048,2048]{1,0:T(8,128)(2,1)} %bitcast.154), kind=kOutput, calls=%fused_computation.1 | convolution fusion | flops 1074003968 | bytes 9437184 | tf_op jit(solution)/shard_map/dot_general | solution.py:81
  288.3 3.8 %all-to-all-done.4 = bf16[4,512,128]{1,2,0:T(8,128)(2,1)S(1)} async-done(((bf16[4,512,128]{1,2,0:T(8,128)(2,1)}), bf16[4,512,128]{1,2,0:T(8,128)(2,1)S(1)}, u32[]{:S(2)}, u32[]{:S(2)}) %all-to-all-start.4) | async-done | bytes 524320 | tf_op jit(solution)/shard_map/all_to_all | solution.py:17
  292.2 3.5 all-to-all-start.15
  295.8 2.0 collective-permute-start.4
  298.0 7.2 %collective-permute-done.4 = bf16[512,128]{0,1:T(8,128)(2,1)S(1)} collective-permute-done((bf16[512,128]{0,1:T(8,128)(2,1)S(1)}, bf16[512,128]{0,1:T(8,128)(2,1)S(1)}, u32[]{:S(2)}, u32[]{:S(2)}) %collective-permute-start.4) | collective-permute-done | bytes 131104 | tf_op jit(solution)/shard_map/ppermute | solution.py:42
  306.6 1.9 collective-permute-start.9
  308.5 10.5 %all_gather.23 = bf16[2048,128]{0,1:T(8,128)(2,1)S(1)} all-gather(bf16[512,128]{0,1:T(8,128)(2,1)S(1)} %fusion.11), channel_id=1, replica_groups=mesh['slab'=8,'row'=4,'col'=4] {'row'}, dimensions={0}, use_global_device_ids=true | all-gather | bytes 655360 | tf_op jit(solution)/shard_map/all_gather | solution.py:76
  320.1 3.5 all-to-all-start.16
  323.6 6.3 %convolution_convert_fusion.6 = bf16[128,2048]{1,0:T(8,128)(2,1)S(1)} fusion(bf16[2048,128]{0,1:T(8,128)(2,1)S(1)} %all_gather.23, bf16[2048,2048]{1,0:T(8,128)(2,1)} %bitcast.155), kind=kOutput, calls=%fused_computation.6 | convolution fusion | flops 1074003968 | bytes 9437184 | tf_op jit(solution)/shard_map/dot_general | solution.py:74
  330.7 3.1 all-to-all-done.16
  333.8 3.5 all-to-all-start.5
  337.3 4.7 %convolution_convert_fusion = bf16[128,2048]{1,0:T(8,128)(2,1)S(1)} fusion(bf16[2048,128]{1,0:T(8,128)(2,1)S(1)} %bitcast.159, bf16[2048,2048]{1,0:T(8,128)(2,1)} %bitcast.156), kind=kOutput, calls=%fused_computation | convolution fusion | flops 1074003968 | bytes 9437184 | tf_op jit(solution)/shard_map/dot_general | solution.py:81
  342.8 3.9 %all-to-all-done.5 = bf16[4,512,128]{1,2,0:T(8,128)(2,1)S(1)} async-done(((bf16[4,512,128]{1,2,0:T(8,128)(2,1)}), bf16[4,512,128]{1,2,0:T(8,128)(2,1)S(1)}, u32[]{:S(2)}, u32[]{:S(2)}) %all-to-all-start.5) | async-done | bytes 524320 | tf_op jit(solution)/shard_map/all_to_all | solution.py:17
  346.6 3.5 all-to-all-start.17
  351.0 9.4 %all-to-all-done.17 = bf16[4,512,128]{1,2,0:T(8,128)(2,1)S(1)} async-done(((bf16[4,512,128]{1,2,0:T(8,128)(2,1)}), bf16[4,512,128]{1,2,0:T(8,128)(2,1)S(1)}, u32[]{:S(2)}, u32[]{:S(2)}) %all-to-all-start.17) | async-done | bytes 524320 | tf_op jit(solution)/shard_map/all_to_all | solution.py:17
  (75 shorter events, 29.3 us)
Async XLA Ops:
  8.6 31.3 %all-to-all-start.6 = ((bf16[4,512,128]{2,1,0:T(8,128)(2,1)}), bf16[4,512,128]{2,1,0:T(8,128)(2,1)S(1)}, u32[]{:S(2)}, u32[]{:S(2)}) async-start(bf16[4,512,128]{2,1,0:T(8,128)(2,1)} %broadcast_in_dim.17), calls=%async_computation.6 | async-start | bytes 1048576 | tf_op jit(solution)/shard_map/all_to_all | solution.py:23
  39.8 14.8 %all-to-all-start = ((bf16[4,512,128]{1,2,0:T(8,128)(2,1)}), bf16[4,512,128]{1,2,0:T(8,128)(2,1)S(1)}, u32[]{:S(2)}, u32[]{:S(2)}) async-start(bf16[4,512,128]{1,2,0:T(8,128)(2,1)} %bitcast.144), calls=%async_computation | async-start | bytes 1048576 | tf_op jit(solution)/shard_map/all_to_all | solution.py:17
  44.7 35.0 %copy-start = (bf16[1,4,512,128]{3,2,1,0:T(8,128)(2,1)S(1)}, bf16[1,4,512,128]{3,2,1,0:T(8,128)(2,1)}, u32[]{:S(2)}) copy-start(bf16[1,4,512,128]{3,2,1,0:T(8,128)(2,1)} %param.5) | copy-start | bytes 1572868
  54.6 30.8 %all-to-all-start.7 = ((bf16[4,512,128]{1,2,0:T(8,128)(2,1)}), bf16[4,512,128]{1,2,0:T(8,128)(2,1)S(1)}, u32[]{:S(2)}, u32[]{:S(2)}) async-start(bf16[4,512,128]{1,2,0:T(8,128)(2,1)} %bitcast.138), calls=%async_computation.7 | async-start | bytes 1048576 | tf_op jit(solution)/shard_map/all_to_all | solution.py:17
  76.7 8.7 %collective-permute-start = (bf16[512,128]{0,1:T(8,128)(2,1)S(1)}, bf16[512,128]{0,1:T(8,128)(2,1)S(1)}, u32[]{:S(2)}, u32[]{:S(2)}) collective-permute-start(bf16[512,128]{0,1:T(8,128)(2,1)S(1)} %reduce_sum.144), channel_id=1, source_target_pairs={{0,16},{16,32},{32,48},{48,64},{64,80},{80,96},{96,112},{1,17},{17... | collective-permute-start | bytes 393224 | tf_op jit(solution)/shard_map/ppermute | solution.py:42
  85.6 13.0 %collective-permute-start.5 = (bf16[512,128]{0,1:T(8,128)(2,1)S(1)}, bf16[512,128]{0,1:T(8,128)(2,1)S(1)}, u32[]{:S(2)}, u32[]{:S(2)}) collective-permute-start(bf16[512,128]{0,1:T(8,128)(2,1)S(1)} %reduce_sum.150), channel_id=1, source_target_pairs={{16,0},{32,16},{48,32},{64,48},{80,64},{96,80},{112,96},{17,1},{33... | collective-permute-start | bytes 393224 | tf_op jit(solution)/shard_map/ppermute | solution.py:42
  99.6 13.7 %all-to-all-start.8 = ((bf16[4,512,128]{2,1,0:T(8,128)(2,1)}), bf16[4,512,128]{2,1,0:T(8,128)(2,1)S(1)}, u32[]{:S(2)}, u32[]{:S(2)}) async-start(bf16[4,512,128]{2,1,0:T(8,128)(2,1)} %broadcast_in_dim.18), calls=%async_computation.8 | async-start | bytes 1048576 | tf_op jit(solution)/shard_map/all_to_all | solution.py:23
  113.3 12.9 %all-to-all-start.1 = ((bf16[4,512,128]{1,2,0:T(8,128)(2,1)}), bf16[4,512,128]{1,2,0:T(8,128)(2,1)S(1)}, u32[]{:S(2)}, u32[]{:S(2)}) async-start(bf16[4,512,128]{1,2,0:T(8,128)(2,1)} %bitcast.143), calls=%async_computation.1 | async-start | bytes 1048576 | tf_op jit(solution)/shard_map/all_to_all | solution.py:17
  126.2 14.3 %all-to-all-start.9 = ((bf16[4,512,128]{1,2,0:T(8,128)(2,1)}), bf16[4,512,128]{1,2,0:T(8,128)(2,1)S(1)}, u32[]{:S(2)}, u32[]{:S(2)}) async-start(bf16[4,512,128]{1,2,0:T(8,128)(2,1)} %bitcast.137), calls=%async_computation.9 | async-start | bytes 1048576 | tf_op jit(solution)/shard_map/all_to_all | solution.py:17
  129.7 9.4 %collective-permute-start.1 = (bf16[512,128]{0,1:T(8,128)(2,1)S(1)}, bf16[512,128]{0,1:T(8,128)(2,1)S(1)}, u32[]{:S(2)}, u32[]{:S(2)}) collective-permute-start(bf16[512,128]{0,1:T(8,128)(2,1)S(1)} %reduce_sum.145), channel_id=1, source_target_pairs={{0,16},{16,32},{32,48},{48,64},{64,80},{80,96},{96,112},{1,17},{17... | collective-permute-start | bytes 393224 | tf_op jit(solution)/shard_map/ppermute | solution.py:42
  140.6 13.7 %collective-permute-start.6 = (bf16[512,128]{0,1:T(8,128)(2,1)S(1)}, bf16[512,128]{0,1:T(8,128)(2,1)S(1)}, u32[]{:S(2)}, u32[]{:S(2)}) collective-permute-start(bf16[512,128]{0,1:T(8,128)(2,1)S(1)} %reduce_sum.151), channel_id=1, source_target_pairs={{16,0},{32,16},{48,32},{64,48},{80,64},{96,80},{112,96},{17,1},{33... | collective-permute-start | bytes 393224 | tf_op jit(solution)/shard_map/ppermute | solution.py:42
  155.4 13.7 %all-to-all-start.10 = ((bf16[4,512,128]{2,1,0:T(8,128)(2,1)}), bf16[4,512,128]{2,1,0:T(8,128)(2,1)S(1)}, u32[]{:S(2)}, u32[]{:S(2)}) async-start(bf16[4,512,128]{2,1,0:T(8,128)(2,1)} %broadcast_in_dim.19), calls=%async_computation.10 | async-start | bytes 1048576 | tf_op jit(solution)/shard_map/all_to_all | solution.py:23
  169.1 12.9 %all-to-all-start.2 = ((bf16[4,512,128]{1,2,0:T(8,128)(2,1)}), bf16[4,512,128]{1,2,0:T(8,128)(2,1)S(1)}, u32[]{:S(2)}, u32[]{:S(2)}) async-start(bf16[4,512,128]{1,2,0:T(8,128)(2,1)} %bitcast.142), calls=%async_computation.2 | async-start | bytes 1048576 | tf_op jit(solution)/shard_map/all_to_all | solution.py:17
  181.9 14.3 %all-to-all-start.11 = ((bf16[4,512,128]{1,2,0:T(8,128)(2,1)}), bf16[4,512,128]{1,2,0:T(8,128)(2,1)S(1)}, u32[]{:S(2)}, u32[]{:S(2)}) async-start(bf16[4,512,128]{1,2,0:T(8,128)(2,1)} %bitcast.136), calls=%async_computation.11 | async-start | bytes 1048576 | tf_op jit(solution)/shard_map/all_to_all | solution.py:17
  185.5 9.4 %collective-permute-start.2 = (bf16[512,128]{0,1:T(8,128)(2,1)S(1)}, bf16[512,128]{0,1:T(8,128)(2,1)S(1)}, u32[]{:S(2)}, u32[]{:S(2)}) collective-permute-start(bf16[512,128]{0,1:T(8,128)(2,1)S(1)} %reduce_sum.146), channel_id=1, source_target_pairs={{0,16},{16,32},{32,48},{48,64},{64,80},{80,96},{96,112},{1,17},{17... | collective-permute-start | bytes 393224 | tf_op jit(solution)/shard_map/ppermute | solution.py:42
  196.4 13.7 %collective-permute-start.7 = (bf16[512,128]{0,1:T(8,128)(2,1)S(1)}, bf16[512,128]{0,1:T(8,128)(2,1)S(1)}, u32[]{:S(2)}, u32[]{:S(2)}) collective-permute-start(bf16[512,128]{0,1:T(8,128)(2,1)S(1)} %reduce_sum.152), channel_id=1, source_target_pairs={{16,0},{32,16},{48,32},{64,48},{80,64},{96,80},{112,96},{17,1},{33... | collective-permute-start | bytes 393224 | tf_op jit(solution)/shard_map/ppermute | solution.py:42
  211.1 13.7 %all-to-all-start.12 = ((bf16[4,512,128]{2,1,0:T(8,128)(2,1)}), bf16[4,512,128]{2,1,0:T(8,128)(2,1)S(1)}, u32[]{:S(2)}, u32[]{:S(2)}) async-start(bf16[4,512,128]{2,1,0:T(8,128)(2,1)} %broadcast_in_dim.20), calls=%async_computation.12 | async-start | bytes 1048576 | tf_op jit(solution)/shard_map/all_to_all | solution.py:23
  224.8 12.9 %all-to-all-start.3 = ((bf16[4,512,128]{1,2,0:T(8,128)(2,1)}), bf16[4,512,128]{1,2,0:T(8,128)(2,1)S(1)}, u32[]{:S(2)}, u32[]{:S(2)}) async-start(bf16[4,512,128]{1,2,0:T(8,128)(2,1)} %bitcast.141), calls=%async_computation.3 | async-start | bytes 1048576 | tf_op jit(solution)/shard_map/all_to_all | solution.py:17
  237.7 14.3 %all-to-all-start.13 = ((bf16[4,512,128]{1,2,0:T(8,128)(2,1)}), bf16[4,512,128]{1,2,0:T(8,128)(2,1)S(1)}, u32[]{:S(2)}, u32[]{:S(2)}) async-start(bf16[4,512,128]{1,2,0:T(8,128)(2,1)} %bitcast.135), calls=%async_computation.13 | async-start | bytes 1048576 | tf_op jit(solution)/shard_map/all_to_all | solution.py:17
  241.3 9.4 %collective-permute-start.3 = (bf16[512,128]{0,1:T(8,128)(2,1)S(1)}, bf16[512,128]{0,1:T(8,128)(2,1)S(1)}, u32[]{:S(2)}, u32[]{:S(2)}) collective-permute-start(bf16[512,128]{0,1:T(8,128)(2,1)S(1)} %reduce_sum.147), channel_id=1, source_target_pairs={{0,16},{16,32},{32,48},{48,64},{64,80},{80,96},{96,112},{1,17},{17... | collective-permute-start | bytes 393224 | tf_op jit(solution)/shard_map/ppermute | solution.py:42
  252.1 12.4 %collective-permute-start.8 = (bf16[512,128]{0,1:T(8,128)(2,1)S(1)}, bf16[512,128]{0,1:T(8,128)(2,1)S(1)}, u32[]{:S(2)}, u32[]{:S(2)}) collective-permute-start(bf16[512,128]{0,1:T(8,128)(2,1)S(1)} %reduce_sum.153), channel_id=1, source_target_pairs={{16,0},{32,16},{48,32},{64,48},{80,64},{96,80},{112,96},{17,1},{33... | collective-permute-start | bytes 393224 | tf_op jit(solution)/shard_map/ppermute | solution.py:42
  265.6 13.7 %all-to-all-start.14 = ((bf16[4,512,128]{2,1,0:T(8,128)(2,1)}), bf16[4,512,128]{2,1,0:T(8,128)(2,1)S(1)}, u32[]{:S(2)}, u32[]{:S(2)}) async-start(bf16[4,512,128]{2,1,0:T(8,128)(2,1)} %broadcast_in_dim.21), calls=%async_computation.14 | async-start | bytes 1048576 | tf_op jit(solution)/shard_map/all_to_all | solution.py:23
  279.3 12.9 %all-to-all-start.4 = ((bf16[4,512,128]{1,2,0:T(8,128)(2,1)}), bf16[4,512,128]{1,2,0:T(8,128)(2,1)S(1)}, u32[]{:S(2)}, u32[]{:S(2)}) async-start(bf16[4,512,128]{1,2,0:T(8,128)(2,1)} %bitcast.140), calls=%async_computation.4 | async-start | bytes 1048576 | tf_op jit(solution)/shard_map/all_to_all | solution.py:17
  292.2 14.3 %all-to-all-start.15 = ((bf16[4,512,128]{1,2,0:T(8,128)(2,1)}), bf16[4,512,128]{1,2,0:T(8,128)(2,1)S(1)}, u32[]{:S(2)}, u32[]{:S(2)}) async-start(bf16[4,512,128]{1,2,0:T(8,128)(2,1)} %bitcast.134), calls=%async_computation.15 | async-start | bytes 1048576 | tf_op jit(solution)/shard_map/all_to_all | solution.py:17
  295.8 9.4 %collective-permute-start.4 = (bf16[512,128]{0,1:T(8,128)(2,1)S(1)}, bf16[512,128]{0,1:T(8,128)(2,1)S(1)}, u32[]{:S(2)}, u32[]{:S(2)}) collective-permute-start(bf16[512,128]{0,1:T(8,128)(2,1)S(1)} %reduce_sum.148), channel_id=1, source_target_pairs={{0,16},{16,32},{32,48},{48,64},{64,80},{80,96},{96,112},{1,17},{17... | collective-permute-start | bytes 393224 | tf_op jit(solution)/shard_map/ppermute | solution.py:42
  306.6 12.4 %collective-permute-start.9 = (bf16[512,128]{0,1:T(8,128)(2,1)S(1)}, bf16[512,128]{0,1:T(8,128)(2,1)S(1)}, u32[]{:S(2)}, u32[]{:S(2)}) collective-permute-start(bf16[512,128]{0,1:T(8,128)(2,1)S(1)} %reduce_sum.154), channel_id=1, source_target_pairs={{16,0},{32,16},{48,32},{64,48},{80,64},{96,80},{112,96},{17,1},{33... | collective-permute-start | bytes 393224 | tf_op jit(solution)/shard_map/ppermute | solution.py:42
  320.1 13.7 %all-to-all-start.16 = ((bf16[4,512,128]{2,1,0:T(8,128)(2,1)}), bf16[4,512,128]{2,1,0:T(8,128)(2,1)S(1)}, u32[]{:S(2)}, u32[]{:S(2)}) async-start(bf16[4,512,128]{2,1,0:T(8,128)(2,1)} %broadcast_in_dim.22), calls=%async_computation.16 | async-start | bytes 1048576 | tf_op jit(solution)/shard_map/all_to_all | solution.py:23
  333.8 12.9 %all-to-all-start.5 = ((bf16[4,512,128]{1,2,0:T(8,128)(2,1)}), bf16[4,512,128]{1,2,0:T(8,128)(2,1)S(1)}, u32[]{:S(2)}, u32[]{:S(2)}) async-start(bf16[4,512,128]{1,2,0:T(8,128)(2,1)} %bitcast.139), calls=%async_computation.5 | async-start | bytes 1048576 | tf_op jit(solution)/shard_map/all_to_all | solution.py:17
  346.6 13.8 %all-to-all-start.17 = ((bf16[4,512,128]{1,2,0:T(8,128)(2,1)}), bf16[4,512,128]{1,2,0:T(8,128)(2,1)S(1)}, u32[]{:S(2)}, u32[]{:S(2)}) async-start(bf16[4,512,128]{1,2,0:T(8,128)(2,1)} %bitcast.133), calls=%async_computation.17 | async-start | bytes 1048576 | tf_op jit(solution)/shard_map/all_to_all | solution.py:17
where the time goes:
time: 363 us; the launch traced here: 361 us
  starting transfers between devices  88.6 us (24%)
  waiting for transfers between devices  87.6 us (24%)
  matrix products  65.7 us (18%)
  blocking collectives  62 us (17%)
  local copies, waits for them, and re-layouts  31.7 us (9%)
  between operations  23.1 us (6%)
    all_gather x6, blocking collectives, per_device(): lax.all_gather(up_in, 'row', axis=0, tiled=True)  62 us
    all_to_all x12, starting transfers between devices, summed_on_arrival(): lax.all_to_all(in_blocks(value, dim, count), axis, 0, 0, tiled=True)  43.3 us
    all_to_all x12, waiting for transfers between devices, summed_on_arrival(): lax.all_to_all(in_blocks(value, dim, count), axis, 0, 0, tiled=True)  38.1 us
    dot_general x6, matrix products, per_device(): jnp.dot(matrix, lax.all_gather(up_in, 'row', axis=0, tiled=True), preferr...  37.6 us
    ppermute x10, waiting for transfers between devices, shifted(): lax.ppermute(value, axis, [(source, source + steps) for source in range(l...  34.2 us
    dot_general x6, matrix products, per_device(): lax.dot_general(matrix, collect(down_in, 'col', 0), (((0,), (0,)), ((), (...  28 us
    ppermute x10, starting transfers between devices, shifted(): lax.ppermute(value, axis, [(source, source + steps) for source in range(l...  23.5 us
    all_to_all x6, starting transfers between devices, from_everyone(): lax.all_to_all(jnp.broadcast_to(value[None], (count, *value.shape)), axis...  21.9 us
  transfers between devices with their start and end apart: 28, of which 21 were waited for; matrix products, arithmetic and copies ran while one was open for 25% of the time, Pallas kernels for 0%

commit v1 on v0

--- a/solution.py
+++ b/solution.py
@@ -73,7 +73,9 @@
         ).astype(jnp.bfloat16)
         forward_partial_value = jnp.dot(
             matrix,
-            lax.all_gather(up_in, "row", axis=0, tiled=True),
+            jnp.concatenate(
+                lax.all_to_all(jnp.stack([up_in] * lax.axis_size("row")), "row", 0, 0), axis=0
+            ),
             preferred_element_type=jnp.float32,
         )
         forward_summed = summed_on_arrival(forward_partial_value.astype(jnp.bfloat16), "col", 0)

time: 363 us -> 376 us (1.036)
  blocking collectives: 62 us -> 0 us
  waiting for transfers between devices: 87.6 us -> 128 us
  starting transfers between devices: 88.6 us -> 115 us
  local copies, waits for them, and re-layouts: 31.7 us -> 37.9 us
    all_gather x6 -> x0, blocking collectives: 62 us -> none  [per_device(): lax.all_gather(up_in, 'row', axis=0, tiled=True)]
    ppermute x10, waiting for transfers between devices: 34.2 us -> 75 us  [shifted(): lax.ppermute(value, axis, [(source, source + steps) for source in range(l...]
    all_to_all x0 -> x6, starting transfers between devices: none -> 23.4 us  [per_device(): lax.all_to_all(jnp.stack([up_in] * lax.axis_size('row')), 'row', 0, 0)]
    all_to_all x0 -> x6, waiting for transfers between devices: none -> 8.07 us  [per_device(): lax.all_to_all(jnp.stack([up_in] * lax.axis_size('row')), 'row', 0, 0)]
    all_to_all x12, waiting for transfers between devices: 38.1 us -> 31.5 us  [summed_on_arrival(): lax.all_to_all(in_blocks(value, dim, count), axis, 0, 0, tiled=True)]
    another operation x0 -> x6, local copies, waits for them, and re-layouts: none -> 5.61 us  [per_device(): jnp.stack([up_in] * lax.axis_size('row'))]
  transfers between devices with their start and end apart: 28 -> 34, of which waited for: 21 -> 32; matrix products, arithmetic and copies ran while one was open for 25% -> 24% of each run, Pallas kernels for 0% -> 0%
where the time goes in v1:
time: 376 us; the launch traced here: 374 us
  waiting for transfers between devices  128 us (34%)
  starting transfers between devices  115 us (31%)
  matrix products  65.8 us (18%)
  local copies, waits for them, and re-layouts  37.9 us (10%)
  between operations  24 us (6%)
    ppermute x10, waiting for transfers between devices, shifted(): lax.ppermute(value, axis, [(source, source + steps) for source in range(l...  75 us
    all_to_all x12, starting transfers between devices, summed_on_arrival(): lax.all_to_all(in_blocks(value, dim, count), axis, 0, 0, tiled=True)  43.4 us
    dot_general x6, matrix products, per_device(): jnp.dot(matrix, jnp.concatenate(lax.all_to_all(jnp.stack([up_in] * lax.ax...  37.8 us
    all_to_all x12, waiting for transfers between devices, summed_on_arrival(): lax.all_to_all(in_blocks(value, dim, count), axis, 0, 0, tiled=True)  31.5 us
    dot_general x6, matrix products, per_device(): lax.dot_general(matrix, collect(down_in, 'col', 0), (((0,), (0,)), ((), (...  28 us
    ppermute x10, starting transfers between devices, shifted(): lax.ppermute(value, axis, [(source, source + steps) for source in range(l...  26.3 us
    all_to_all x6, starting transfers between devices, per_device(): lax.all_to_all(jnp.stack([up_in] * lax.axis_size('row')), 'row', 0, 0)  23.4 us
    all_to_all x6, starting transfers between devices, from_everyone(): lax.all_to_all(jnp.broadcast_to(value[None], (count, *value.shape)), axis...  21.9 us
  transfers between devices with their start and end apart: 34, of which 32 were waited for; matrix products, arithmetic and copies ran while one was open for 24% of the time, Pallas kernels for 0%

profile of v1, /device:TPU:16, one launch (start us, length us, event | category | flops | bytes accessed | tf_op | source)
XLA Modules:
  0.0 373.5 jit_solution(11757599754837230832)
XLA Ops:
  9.0 5.1 %all-to-all-start = ((bf16[4,512,128]{2,1,0:T(8,128)(2,1)}), bf16[4,512,128]{2,1,0:T(8,128)(2,1)S(1)}, u32[]{:S(2)}, u32[]{:S(2)}) async-start(bf16[4,512,128]{2,1,0:T(8,128)(2,1)} %stack.12), calls=%async_computation | async-start | bytes 1048576 | tf_op jit(solution)/shard_map/all_to_all | solution.py:77
  14.2 10.3 %copy.86 = bf16[256,8,4,512]{3,1,2,0:T(8,128)(2,1)} copy(bf16[256,8,4,512]{3,2,1,0:T(4,128)(2,1)} %bitcast.163) | data formatting | bytes 16777216
  25.4 4.3 %all-to-all-start.12 = ((bf16[4,512,128]{2,1,0:T(8,128)(2,1)}), bf16[4,512,128]{2,1,0:T(8,128)(2,1)S(1)}, u32[]{:S(2)}, u32[]{:S(2)}) async-start(bf16[4,512,128]{2,1,0:T(8,128)(2,1)} %broadcast_in_dim.17), calls=%async_computation.12 | async-start | bytes 1048576 | tf_op jit(solution)/shard_map/all_to_all | solution.py:23
  29.7 6.3 %convolution_convert_fusion.11 = bf16[128,2048]{1,0:T(8,128)(2,1)S(1)} fusion(bf16[2048,128]{1,0:T(8,128)(2,1)S(1)} %bitcast.175, bf16[2048,2048]{1,0:T(8,128)(2,1)} %bitcast.151), kind=kOutput, calls=%fused_computation.11 | convolution fusion | flops 1074003968 | bytes 9437184 | tf_op jit(solution)/shard_map/dot_general | solution.py:74
  36.9 3.0 all-to-all-done.12
  39.8 3.5 all-to-all-start.1
  43.3 4.7 %convolution_convert_fusion.5 = bf16[128,2048]{1,0:T(8,128)(2,1)S(1)} fusion(bf16[2048,128]{1,0:T(8,128)(2,1)S(1)} %bitcast.165, bf16[2048,2048]{1,0:T(8,128)(2,1)} %bitcast.152), kind=kOutput, calls=%fused_computation.5 | convolution fusion | flops 1074003968 | bytes 9437184 | tf_op jit(solution)/shard_map/dot_general | solution.py:83
  49.0 3.6 all-to-all-done.1
  52.5 4.0 %all-to-all-start.13 = ((bf16[4,512,128]{1,2,0:T(8,128)(2,1)}), bf16[4,512,128]{1,2,0:T(8,128)(2,1)S(1)}, u32[]{:S(2)}, u32[]{:S(2)}) async-start(bf16[4,512,128]{1,2,0:T(8,128)(2,1)} %bitcast.144), calls=%async_computation.13 | async-start | bytes 1048576 | tf_op jit(solution)/shard_map/all_to_all | solution.py:17
  75.5 2.9 collective-permute-start
  78.7 5.5 %collective-permute-done = bf16[512,128]{0,1:T(8,128)(2,1)S(1)} collective-permute-done((bf16[512,128]{0,1:T(8,128)(2,1)S(1)}, bf16[512,128]{0,1:T(8,128)(2,1)S(1)}, u32[]{:S(2)}, u32[]{:S(2)}) %collective-permute-start) | collective-permute-done | bytes 131104 | tf_op jit(solution)/shard_map/ppermute | solution.py:42
  85.3 4.4 %all-to-all-start.2 = ((bf16[4,512,128]{2,1,0:T(8,128)(2,1)}), bf16[4,512,128]{2,1,0:T(8,128)(2,1)S(1)}, u32[]{:S(2)}, u32[]{:S(2)}) async-start(bf16[4,512,128]{2,1,0:T(8,128)(2,1)} %stack.13), calls=%async_computation.2 | async-start | bytes 1048576 | tf_op jit(solution)/shard_map/all_to_all | solution.py:77
  91.9 8.0 %collective-permute-done.5 = bf16[512,128]{0,1:T(8,128)(2,1)S(1)} collective-permute-done((bf16[512,128]{0,1:T(8,128)(2,1)S(1)}, bf16[512,128]{0,1:T(8,128)(2,1)S(1)}, u32[]{:S(2)}, u32[]{:S(2)}) %collective-permute-start.5) | collective-permute-done | bytes 131104 | tf_op jit(solution)/shard_map/ppermute | solution.py:42
  100.0 2.8 all-to-all-done.2
  103.7 3.5 all-to-all-start.14
  107.2 6.3 %convolution_convert_fusion.10 = bf16[128,2048]{1,0:T(8,128)(2,1)S(1)} fusion(bf16[2048,128]{1,0:T(8,128)(2,1)S(1)} %bitcast.171, bf16[2048,2048]{1,0:T(8,128)(2,1)} %bitcast.153), kind=kOutput, calls=%fused_computation.10 | convolution fusion | flops 1074003968 | bytes 9437184 | tf_op jit(solution)/shard_map/dot_general | solution.py:74
  116.6 3.6 all-to-all-start.3
  120.3 4.7 %convolution_convert_fusion.4 = bf16[128,2048]{1,0:T(8,128)(2,1)S(1)} fusion(bf16[2048,128]{1,0:T(8,128)(2,1)S(1)} %bitcast.166, bf16[2048,2048]{1,0:T(8,128)(2,1)} %bitcast.154), kind=kOutput, calls=%fused_computation.4 | convolution fusion | flops 1074003968 | bytes 9437184 | tf_op jit(solution)/shard_map/dot_general | solution.py:83
  125.8 2.6 all-to-all-done.3
  128.4 3.5 all-to-all-start.15
  134.0 7.4 %collective-permute-done.1 = bf16[512,128]{0,1:T(8,128)(2,1)S(1)} collective-permute-done((bf16[512,128]{0,1:T(8,128)(2,1)S(1)}, bf16[512,128]{0,1:T(8,128)(2,1)S(1)}, u32[]{:S(2)}, u32[]{:S(2)}) %collective-permute-start.1) | collective-permute-done | bytes 131104 | tf_op jit(solution)/shard_map/ppermute | solution.py:42
  143.6 3.5 all-to-all-start.4
  147.2 3.4 collective-permute-start.6
  150.8 8.0 %collective-permute-done.6 = bf16[512,128]{0,1:T(8,128)(2,1)S(1)} collective-permute-done((bf16[512,128]{0,1:T(8,128)(2,1)S(1)}, bf16[512,128]{0,1:T(8,128)(2,1)S(1)}, u32[]{:S(2)}, u32[]{:S(2)}) %collective-permute-start.6) | collective-permute-done | bytes 131104 | tf_op jit(solution)/shard_map/ppermute | solution.py:42
  161.1 3.5 all-to-all-start.16
  164.6 6.3 %convolution_convert_fusion.9 = bf16[128,2048]{1,0:T(8,128)(2,1)S(1)} fusion(bf16[2048,128]{1,0:T(8,128)(2,1)S(1)} %bitcast.172, bf16[2048,2048]{1,0:T(8,128)(2,1)} %bitcast.155), kind=kOutput, calls=%fused_computation.9 | convolution fusion | flops 1074003968 | bytes 9437184 | tf_op jit(solution)/shard_map/dot_general | solution.py:74
  171.8 2.2 all-to-all-done.16
  174.0 3.5 all-to-all-start.5
  177.5 4.7 %convolution_convert_fusion.3 = bf16[128,2048]{1,0:T(8,128)(2,1)S(1)} fusion(bf16[2048,128]{1,0:T(8,128)(2,1)S(1)} %bitcast.167, bf16[2048,2048]{1,0:T(8,128)(2,1)} %bitcast.156), kind=kOutput, calls=%fused_computation.3 | convolution fusion | flops 1074003968 | bytes 9437184 | tf_op jit(solution)/shard_map/dot_general | solution.py:83
  183.0 2.8 all-to-all-done.5
  185.7 3.7 all-to-all-start.17
  191.6 7.4 %collective-permute-done.2 = bf16[512,128]{0,1:T(8,128)(2,1)S(1)} collective-permute-done((bf16[512,128]{0,1:T(8,128)(2,1)S(1)}, bf16[512,128]{0,1:T(8,128)(2,1)S(1)}, u32[]{:S(2)}, u32[]{:S(2)}) %collective-permute-start.2) | collective-permute-done | bytes 131104 | tf_op jit(solution)/shard_map/ppermute | solution.py:42
  201.3 3.5 all-to-all-start.6
  204.8 3.4 collective-permute-start.7
  208.4 8.0 %collective-permute-done.7 = bf16[512,128]{0,1:T(8,128)(2,1)S(1)} collective-permute-done((bf16[512,128]{0,1:T(8,128)(2,1)S(1)}, bf16[512,128]{0,1:T(8,128)(2,1)S(1)}, u32[]{:S(2)}, u32[]{:S(2)}) %collective-permute-start.7) | collective-permute-done | bytes 131104 | tf_op jit(solution)/shard_map/ppermute | solution.py:42
  218.7 3.5 all-to-all-start.18
  222.2 6.3 %convolution_convert_fusion.8 = bf16[128,2048]{1,0:T(8,128)(2,1)S(1)} fusion(bf16[2048,128]{1,0:T(8,128)(2,1)S(1)} %bitcast.173, bf16[2048,2048]{1,0:T(8,128)(2,1)} %bitcast.157), kind=kOutput, calls=%fused_computation.8 | convolution fusion | flops 1074003968 | bytes 9437184 | tf_op jit(solution)/shard_map/dot_general | solution.py:74
  229.4 2.2 all-to-all-done.18
  231.6 3.5 all-to-all-start.7
  235.1 4.7 %convolution_convert_fusion.2 = bf16[128,2048]{1,0:T(8,128)(2,1)S(1)} fusion(bf16[2048,128]{1,0:T(8,128)(2,1)S(1)} %bitcast.168, bf16[2048,2048]{1,0:T(8,128)(2,1)} %bitcast.158), kind=kOutput, calls=%fused_computation.2 | convolution fusion | flops 1074003968 | bytes 9437184 | tf_op jit(solution)/shard_map/dot_general | solution.py:83
  240.6 2.8 all-to-all-done.7
  243.4 3.7 all-to-all-start.19
  249.2 7.4 %collective-permute-done.3 = bf16[512,128]{0,1:T(8,128)(2,1)S(1)} collective-permute-done((bf16[512,128]{0,1:T(8,128)(2,1)S(1)}, bf16[512,128]{0,1:T(8,128)(2,1)S(1)}, u32[]{:S(2)}, u32[]{:S(2)}) %collective-permute-start.3) | collective-permute-done | bytes 131104 | tf_op jit(solution)/shard_map/ppermute | solution.py:42
  258.9 3.5 all-to-all-start.8
  262.5 3.4 collective-permute-start.8
  266.0 8.0 %collective-permute-done.8 = bf16[512,128]{0,1:T(8,128)(2,1)S(1)} collective-permute-done((bf16[512,128]{0,1:T(8,128)(2,1)S(1)}, bf16[512,128]{0,1:T(8,128)(2,1)S(1)}, u32[]{:S(2)}, u32[]{:S(2)}) %collective-permute-start.8) | collective-permute-done | bytes 131104 | tf_op jit(solution)/shard_map/ppermute | solution.py:42
  276.3 3.7 all-to-all-start.20
  280.0 6.3 %convolution_convert_fusion.7 = bf16[128,2048]{1,0:T(8,128)(2,1)S(1)} fusion(bf16[2048,128]{1,0:T(8,128)(2,1)S(1)} %bitcast.174, bf16[2048,2048]{1,0:T(8,128)(2,1)} %bitcast.159), kind=kOutput, calls=%fused_computation.7 | convolution fusion | flops 1074003968 | bytes 9437184 | tf_op jit(solution)/shard_map/dot_general | solution.py:74
  289.2 3.5 all-to-all-start.9
  292.7 4.7 %convolution_convert_fusion.1 = bf16[128,2048]{1,0:T(8,128)(2,1)S(1)} fusion(bf16[2048,128]{1,0:T(8,128)(2,1)S(1)} %bitcast.169, bf16[2048,2048]{1,0:T(8,128)(2,1)} %bitcast.160), kind=kOutput, calls=%fused_computation.1 | convolution fusion | flops 1074003968 | bytes 9437184 | tf_op jit(solution)/shard_map/dot_general | solution.py:83
  298.2 2.8 all-to-all-done.9
  301.0 3.7 all-to-all-start.21
  306.9 7.4 %collective-permute-done.4 = bf16[512,128]{0,1:T(8,128)(2,1)S(1)} collective-permute-done((bf16[512,128]{0,1:T(8,128)(2,1)S(1)}, bf16[512,128]{0,1:T(8,128)(2,1)S(1)}, u32[]{:S(2)}, u32[]{:S(2)}) %collective-permute-start.4) | collective-permute-done | bytes 131104 | tf_op jit(solution)/shard_map/ppermute | solution.py:42
  316.5 3.5 all-to-all-start.10
  320.1 3.4 collective-permute-start.9
  323.7 8.0 %collective-permute-done.9 = bf16[512,128]{0,1:T(8,128)(2,1)S(1)} collective-permute-done((bf16[512,128]{0,1:T(8,128)(2,1)S(1)}, bf16[512,128]{0,1:T(8,128)(2,1)S(1)}, u32[]{:S(2)}, u32[]{:S(2)}) %collective-permute-start.9) | collective-permute-done | bytes 131104 | tf_op jit(solution)/shard_map/ppermute | solution.py:42
  334.0 3.5 all-to-all-start.22
  337.5 6.3 %convolution_convert_fusion.6 = bf16[128,2048]{1,0:T(8,128)(2,1)S(1)} fusion(bf16[2048,128]{1,0:T(8,128)(2,1)S(1)} %bitcast.170, bf16[2048,2048]{1,0:T(8,128)(2,1)} %bitcast.161), kind=kOutput, calls=%fused_computation.6 | convolution fusion | flops 1074003968 | bytes 9437184 | tf_op jit(solution)/shard_map/dot_general | solution.py:74
  344.7 2.2 all-to-all-done.22
  346.9 3.5 all-to-all-start.11
  350.4 4.7 %convolution_convert_fusion = bf16[128,2048]{1,0:T(8,128)(2,1)S(1)} fusion(bf16[2048,128]{1,0:T(8,128)(2,1)S(1)} %bitcast.164, bf16[2048,2048]{1,0:T(8,128)(2,1)} %bitcast.162), kind=kOutput, calls=%fused_computation | convolution fusion | flops 1074003968 | bytes 9437184 | tf_op jit(solution)/shard_map/dot_general | solution.py:83
  355.9 2.8 all-to-all-done.11
  358.6 3.7 all-to-all-start.23
  363.2 9.5 %all-to-all-done.23 = bf16[4,512,128]{1,2,0:T(8,128)(2,1)S(1)} async-done(((bf16[4,512,128]{1,2,0:T(8,128)(2,1)}), bf16[4,512,128]{1,2,0:T(8,128)(2,1)S(1)}, u32[]{:S(2)}, u32[]{:S(2)}) %all-to-all-start.23) | async-done | bytes 524320 | tf_op jit(solution)/shard_map/all_to_all | solution.py:17
  (92 shorter events, 53.9 us)
Async XLA Ops:
  9.0 15.5 %all-to-all-start = ((bf16[4,512,128]{2,1,0:T(8,128)(2,1)}), bf16[4,512,128]{2,1,0:T(8,128)(2,1)S(1)}, u32[]{:S(2)}, u32[]{:S(2)}) async-start(bf16[4,512,128]{2,1,0:T(8,128)(2,1)} %stack.12), calls=%async_computation | async-start | bytes 1048576 | tf_op jit(solution)/shard_map/all_to_all | solution.py:77
  25.4 14.4 %all-to-all-start.12 = ((bf16[4,512,128]{2,1,0:T(8,128)(2,1)}), bf16[4,512,128]{2,1,0:T(8,128)(2,1)S(1)}, u32[]{:S(2)}, u32[]{:S(2)}) async-start(bf16[4,512,128]{2,1,0:T(8,128)(2,1)} %broadcast_in_dim.17), calls=%async_computation.12 | async-start | bytes 1048576 | tf_op jit(solution)/shard_map/all_to_all | solution.py:23
  39.8 12.7 %all-to-all-start.1 = ((bf16[4,512,128]{1,2,0:T(8,128)(2,1)}), bf16[4,512,128]{1,2,0:T(8,128)(2,1)S(1)}, u32[]{:S(2)}, u32[]{:S(2)}) async-start(bf16[4,512,128]{1,2,0:T(8,128)(2,1)} %bitcast.150), calls=%async_computation.1 | async-start | bytes 1048576 | tf_op jit(solution)/shard_map/all_to_all | solution.py:17
  43.3 35.1 %copy-start = (bf16[1,4,512,128]{3,2,1,0:T(8,128)(2,1)S(1)}, bf16[1,4,512,128]{3,2,1,0:T(8,128)(2,1)}, u32[]{:S(2)}) copy-start(bf16[1,4,512,128]{3,2,1,0:T(8,128)(2,1)} %param.5) | copy-start | bytes 1572868
  52.5 31.8 %all-to-all-start.13 = ((bf16[4,512,128]{1,2,0:T(8,128)(2,1)}), bf16[4,512,128]{1,2,0:T(8,128)(2,1)S(1)}, u32[]{:S(2)}, u32[]{:S(2)}) async-start(bf16[4,512,128]{1,2,0:T(8,128)(2,1)} %bitcast.144), calls=%async_computation.13 | async-start | bytes 1048576 | tf_op jit(solution)/shard_map/all_to_all | solution.py:17
  75.5 8.7 %collective-permute-start = (bf16[512,128]{0,1:T(8,128)(2,1)S(1)}, bf16[512,128]{0,1:T(8,128)(2,1)S(1)}, u32[]{:S(2)}, u32[]{:S(2)}) collective-permute-start(bf16[512,128]{0,1:T(8,128)(2,1)S(1)} %reduce_sum.144), channel_id=1, source_target_pairs={{0,16},{16,32},{32,48},{48,64},{64,80},{80,96},{96,112},{1,17},{17... | collective-permute-start | bytes 393224 | tf_op jit(solution)/shard_map/ppermute | solution.py:42
  85.3 17.5 %all-to-all-start.2 = ((bf16[4,512,128]{2,1,0:T(8,128)(2,1)}), bf16[4,512,128]{2,1,0:T(8,128)(2,1)S(1)}, u32[]{:S(2)}, u32[]{:S(2)}) async-start(bf16[4,512,128]{2,1,0:T(8,128)(2,1)} %stack.13), calls=%async_computation.2 | async-start | bytes 1048576 | tf_op jit(solution)/shard_map/all_to_all | solution.py:77
  89.8 10.0 %collective-permute-start.5 = (bf16[512,128]{0,1:T(8,128)(2,1)S(1)}, bf16[512,128]{0,1:T(8,128)(2,1)S(1)}, u32[]{:S(2)}, u32[]{:S(2)}) collective-permute-start(bf16[512,128]{0,1:T(8,128)(2,1)S(1)} %reduce_sum.150), channel_id=1, source_target_pairs={{16,0},{32,16},{48,32},{64,48},{80,64},{96,80},{112,96},{17,1},{33... | collective-permute-start | bytes 393224 | tf_op jit(solution)/shard_map/ppermute | solution.py:42
  103.7 12.9 %all-to-all-start.14 = ((bf16[4,512,128]{2,1,0:T(8,128)(2,1)}), bf16[4,512,128]{2,1,0:T(8,128)(2,1)S(1)}, u32[]{:S(2)}, u32[]{:S(2)}) async-start(bf16[4,512,128]{2,1,0:T(8,128)(2,1)} %broadcast_in_dim.18), calls=%async_computation.14 | async-start | bytes 1048576 | tf_op jit(solution)/shard_map/all_to_all | solution.py:23
  116.6 11.8 %all-to-all-start.3 = ((bf16[4,512,128]{1,2,0:T(8,128)(2,1)}), bf16[4,512,128]{1,2,0:T(8,128)(2,1)S(1)}, u32[]{:S(2)}, u32[]{:S(2)}) async-start(bf16[4,512,128]{1,2,0:T(8,128)(2,1)} %bitcast.149), calls=%async_computation.3 | async-start | bytes 1048576 | tf_op jit(solution)/shard_map/all_to_all | solution.py:17
  128.4 14.3 %all-to-all-start.15 = ((bf16[4,512,128]{1,2,0:T(8,128)(2,1)}), bf16[4,512,128]{1,2,0:T(8,128)(2,1)S(1)}, u32[]{:S(2)}, u32[]{:S(2)}) async-start(bf16[4,512,128]{1,2,0:T(8,128)(2,1)} %bitcast.143), calls=%async_computation.15 | async-start | bytes 1048576 | tf_op jit(solution)/shard_map/all_to_all | solution.py:17
  131.9 9.4 %collective-permute-start.1 = (bf16[512,128]{0,1:T(8,128)(2,1)S(1)}, bf16[512,128]{0,1:T(8,128)(2,1)S(1)}, u32[]{:S(2)}, u32[]{:S(2)}) collective-permute-start(bf16[512,128]{0,1:T(8,128)(2,1)S(1)} %reduce_sum.145), channel_id=1, source_target_pairs={{0,16},{16,32},{32,48},{48,64},{64,80},{80,96},{96,112},{1,17},{17... | collective-permute-start | bytes 393224 | tf_op jit(solution)/shard_map/ppermute | solution.py:42
  143.6 16.6 %all-to-all-start.4 = ((bf16[4,512,128]{2,1,0:T(8,128)(2,1)}), bf16[4,512,128]{2,1,0:T(8,128)(2,1)S(1)}, u32[]{:S(2)}, u32[]{:S(2)}) async-start(bf16[4,512,128]{2,1,0:T(8,128)(2,1)} %stack.14), calls=%async_computation.4 | async-start | bytes 1048576 | tf_op jit(solution)/shard_map/all_to_all | solution.py:77
  147.2 11.5 %collective-permute-start.6 = (bf16[512,128]{0,1:T(8,128)(2,1)S(1)}, bf16[512,128]{0,1:T(8,128)(2,1)S(1)}, u32[]{:S(2)}, u32[]{:S(2)}) collective-permute-start(bf16[512,128]{0,1:T(8,128)(2,1)S(1)} %reduce_sum.151), channel_id=1, source_target_pairs={{16,0},{32,16},{48,32},{64,48},{80,64},{96,80},{112,96},{17,1},{33... | collective-permute-start | bytes 393224 | tf_op jit(solution)/shard_map/ppermute | solution.py:42
  161.1 12.9 %all-to-all-start.16 = ((bf16[4,512,128]{2,1,0:T(8,128)(2,1)}), bf16[4,512,128]{2,1,0:T(8,128)(2,1)S(1)}, u32[]{:S(2)}, u32[]{:S(2)}) async-start(bf16[4,512,128]{2,1,0:T(8,128)(2,1)} %broadcast_in_dim.19), calls=%async_computation.16 | async-start | bytes 1048576 | tf_op jit(solution)/shard_map/all_to_all | solution.py:23
  174.0 11.8 %all-to-all-start.5 = ((bf16[4,512,128]{1,2,0:T(8,128)(2,1)}), bf16[4,512,128]{1,2,0:T(8,128)(2,1)S(1)}, u32[]{:S(2)}, u32[]{:S(2)}) async-start(bf16[4,512,128]{1,2,0:T(8,128)(2,1)} %bitcast.148), calls=%async_computation.5 | async-start | bytes 1048576 | tf_op jit(solution)/shard_map/all_to_all | solution.py:17
  185.7 14.6 %all-to-all-start.17 = ((bf16[4,512,128]{1,2,0:T(8,128)(2,1)}), bf16[4,512,128]{1,2,0:T(8,128)(2,1)S(1)}, u32[]{:S(2)}, u32[]{:S(2)}) async-start(bf16[4,512,128]{1,2,0:T(8,128)(2,1)} %bitcast.142), calls=%async_computation.17 | async-start | bytes 1048576 | tf_op jit(solution)/shard_map/all_to_all | solution.py:17
  189.5 9.5 %collective-permute-start.2 = (bf16[512,128]{0,1:T(8,128)(2,1)S(1)}, bf16[512,128]{0,1:T(8,128)(2,1)S(1)}, u32[]{:S(2)}, u32[]{:S(2)}) collective-permute-start(bf16[512,128]{0,1:T(8,128)(2,1)S(1)} %reduce_sum.146), channel_id=1, source_target_pairs={{0,16},{16,32},{32,48},{48,64},{64,80},{80,96},{96,112},{1,17},{17... | collective-permute-start | bytes 393224 | tf_op jit(solution)/shard_map/ppermute | solution.py:42
  201.3 16.6 %all-to-all-start.6 = ((bf16[4,512,128]{2,1,0:T(8,128)(2,1)}), bf16[4,512,128]{2,1,0:T(8,128)(2,1)S(1)}, u32[]{:S(2)}, u32[]{:S(2)}) async-start(bf16[4,512,128]{2,1,0:T(8,128)(2,1)} %stack.15), calls=%async_computation.6 | async-start | bytes 1048576 | tf_op jit(solution)/shard_map/all_to_all | solution.py:77
  204.8 11.5 %collective-permute-start.7 = (bf16[512,128]{0,1:T(8,128)(2,1)S(1)}, bf16[512,128]{0,1:T(8,128)(2,1)S(1)}, u32[]{:S(2)}, u32[]{:S(2)}) collective-permute-start(bf16[512,128]{0,1:T(8,128)(2,1)S(1)} %reduce_sum.152), channel_id=1, source_target_pairs={{16,0},{32,16},{48,32},{64,48},{80,64},{96,80},{112,96},{17,1},{33... | collective-permute-start | bytes 393224 | tf_op jit(solution)/shard_map/ppermute | solution.py:42
  218.7 12.9 %all-to-all-start.18 = ((bf16[4,512,128]{2,1,0:T(8,128)(2,1)}), bf16[4,512,128]{2,1,0:T(8,128)(2,1)S(1)}, u32[]{:S(2)}, u32[]{:S(2)}) async-start(bf16[4,512,128]{2,1,0:T(8,128)(2,1)} %broadcast_in_dim.20), calls=%async_computation.18 | async-start | bytes 1048576 | tf_op jit(solution)/shard_map/all_to_all | solution.py:23
  231.6 11.8 %all-to-all-start.7 = ((bf16[4,512,128]{1,2,0:T(8,128)(2,1)}), bf16[4,512,128]{1,2,0:T(8,128)(2,1)S(1)}, u32[]{:S(2)}, u32[]{:S(2)}) async-start(bf16[4,512,128]{1,2,0:T(8,128)(2,1)} %bitcast.147), calls=%async_computation.7 | async-start | bytes 1048576 | tf_op jit(solution)/shard_map/all_to_all | solution.py:17
  243.4 14.6 %all-to-all-start.19 = ((bf16[4,512,128]{1,2,0:T(8,128)(2,1)}), bf16[4,512,128]{1,2,0:T(8,128)(2,1)S(1)}, u32[]{:S(2)}, u32[]{:S(2)}) async-start(bf16[4,512,128]{1,2,0:T(8,128)(2,1)} %bitcast.141), calls=%async_computation.19 | async-start | bytes 1048576 | tf_op jit(solution)/shard_map/all_to_all | solution.py:17
  247.2 9.5 %collective-permute-start.3 = (bf16[512,128]{0,1:T(8,128)(2,1)S(1)}, bf16[512,128]{0,1:T(8,128)(2,1)S(1)}, u32[]{:S(2)}, u32[]{:S(2)}) collective-permute-start(bf16[512,128]{0,1:T(8,128)(2,1)S(1)} %reduce_sum.147), channel_id=1, source_target_pairs={{0,16},{16,32},{32,48},{48,64},{64,80},{80,96},{96,112},{1,17},{17... | collective-permute-start | bytes 393224 | tf_op jit(solution)/shard_map/ppermute | solution.py:42
  258.9 16.6 %all-to-all-start.8 = ((bf16[4,512,128]{2,1,0:T(8,128)(2,1)}), bf16[4,512,128]{2,1,0:T(8,128)(2,1)S(1)}, u32[]{:S(2)}, u32[]{:S(2)}) async-start(bf16[4,512,128]{2,1,0:T(8,128)(2,1)} %stack.16), calls=%async_computation.8 | async-start | bytes 1048576 | tf_op jit(solution)/shard_map/all_to_all | solution.py:77
  262.5 11.5 %collective-permute-start.8 = (bf16[512,128]{0,1:T(8,128)(2,1)S(1)}, bf16[512,128]{0,1:T(8,128)(2,1)S(1)}, u32[]{:S(2)}, u32[]{:S(2)}) collective-permute-start(bf16[512,128]{0,1:T(8,128)(2,1)S(1)} %reduce_sum.153), channel_id=1, source_target_pairs={{16,0},{32,16},{48,32},{64,48},{80,64},{96,80},{112,96},{17,1},{33... | collective-permute-start | bytes 393224 | tf_op jit(solution)/shard_map/ppermute | solution.py:42
  276.3 12.9 %all-to-all-start.20 = ((bf16[4,512,128]{2,1,0:T(8,128)(2,1)}), bf16[4,512,128]{2,1,0:T(8,128)(2,1)S(1)}, u32[]{:S(2)}, u32[]{:S(2)}) async-start(bf16[4,512,128]{2,1,0:T(8,128)(2,1)} %broadcast_in_dim.21), calls=%async_computation.20 | async-start | bytes 1048576 | tf_op jit(solution)/shard_map/all_to_all | solution.py:23
  289.2 11.8 %all-to-all-start.9 = ((bf16[4,512,128]{1,2,0:T(8,128)(2,1)}), bf16[4,512,128]{1,2,0:T(8,128)(2,1)S(1)}, u32[]{:S(2)}, u32[]{:S(2)}) async-start(bf16[4,512,128]{1,2,0:T(8,128)(2,1)} %bitcast.146), calls=%async_computation.9 | async-start | bytes 1048576 | tf_op jit(solution)/shard_map/all_to_all | solution.py:17
  301.0 14.6 %all-to-all-start.21 = ((bf16[4,512,128]{1,2,0:T(8,128)(2,1)}), bf16[4,512,128]{1,2,0:T(8,128)(2,1)S(1)}, u32[]{:S(2)}, u32[]{:S(2)}) async-start(bf16[4,512,128]{1,2,0:T(8,128)(2,1)} %bitcast.140), calls=%async_computation.21 | async-start | bytes 1048576 | tf_op jit(solution)/shard_map/all_to_all | solution.py:17
  304.8 9.5 %collective-permute-start.4 = (bf16[512,128]{0,1:T(8,128)(2,1)S(1)}, bf16[512,128]{0,1:T(8,128)(2,1)S(1)}, u32[]{:S(2)}, u32[]{:S(2)}) collective-permute-start(bf16[512,128]{0,1:T(8,128)(2,1)S(1)} %reduce_sum.148), channel_id=1, source_target_pairs={{0,16},{16,32},{32,48},{48,64},{64,80},{80,96},{96,112},{1,17},{17... | collective-permute-start | bytes 393224 | tf_op jit(solution)/shard_map/ppermute | solution.py:42
  316.5 16.6 %all-to-all-start.10 = ((bf16[4,512,128]{2,1,0:T(8,128)(2,1)}), bf16[4,512,128]{2,1,0:T(8,128)(2,1)S(1)}, u32[]{:S(2)}, u32[]{:S(2)}) async-start(bf16[4,512,128]{2,1,0:T(8,128)(2,1)} %stack.17), calls=%async_computation.10 | async-start | bytes 1048576 | tf_op jit(solution)/shard_map/all_to_all | solution.py:77
  320.1 11.5 %collective-permute-start.9 = (bf16[512,128]{0,1:T(8,128)(2,1)S(1)}, bf16[512,128]{0,1:T(8,128)(2,1)S(1)}, u32[]{:S(2)}, u32[]{:S(2)}) collective-permute-start(bf16[512,128]{0,1:T(8,128)(2,1)S(1)} %reduce_sum.154), channel_id=1, source_target_pairs={{16,0},{32,16},{48,32},{64,48},{80,64},{96,80},{112,96},{17,1},{33... | collective-permute-start | bytes 393224 | tf_op jit(solution)/shard_map/ppermute | solution.py:42
  334.0 12.9 %all-to-all-start.22 = ((bf16[4,512,128]{2,1,0:T(8,128)(2,1)}), bf16[4,512,128]{2,1,0:T(8,128)(2,1)S(1)}, u32[]{:S(2)}, u32[]{:S(2)}) async-start(bf16[4,512,128]{2,1,0:T(8,128)(2,1)} %broadcast_in_dim.22), calls=%async_computation.22 | async-start | bytes 1048576 | tf_op jit(solution)/shard_map/all_to_all | solution.py:23
  346.9 11.8 %all-to-all-start.11 = ((bf16[4,512,128]{1,2,0:T(8,128)(2,1)}), bf16[4,512,128]{1,2,0:T(8,128)(2,1)S(1)}, u32[]{:S(2)}, u32[]{:S(2)}) async-start(bf16[4,512,128]{1,2,0:T(8,128)(2,1)} %bitcast.145), calls=%async_computation.11 | async-start | bytes 1048576 | tf_op jit(solution)/shard_map/all_to_all | solution.py:17
  358.6 14.0 %all-to-all-start.23 = ((bf16[4,512,128]{1,2,0:T(8,128)(2,1)}), bf16[4,512,128]{1,2,0:T(8,128)(2,1)S(1)}, u32[]{:S(2)}, u32[]{:S(2)}) async-start(bf16[4,512,128]{1,2,0:T(8,128)(2,1)} %bitcast.139), calls=%async_computation.23 | async-start | bytes 1048576 | tf_op jit(solution)/shard_map/all_to_all | solution.py:17
